TPU v7x, 512 devices: a whole 4x4x16 slice. The times are simulated.
512 devices in a mesh: region: 4 (over z_hi), dom: 128 (over x, y, z_lo, core).
Axes of the slice: x: 4, y: 4, z: 16 (z_hi: 4, z_lo: 4; z = z_hi * 4 + z_lo), core: 2. Of those that a mesh axis runs over, the one named last changes fastest.
Arguments:
- entity: float32 [400, 65536], P(None, 'dom'), may hold values from -3 to 3
- relation: float32 [400, 256], replicated, may hold values from -3.6 to 3.6
- head_index: int32 [262144], P(('region', 'dom')), may hold values from 0 to 511
- relation_index: int32 [262144], P(('region', 'dom')), may hold values from 0 to 255
- tail_index: int32 [262144], P(('region', 'dom')), may hold values from 0 to 511
- negative_index: int32 [589824], P(('region', 'dom')), may hold values from 0 to 511
- plan: int32 [1], replicated, may hold values from 1 to 127
- edge_count: int32 [512], P(('region', 'dom')), may hold values from 128 to 512, as said below
Outputs:
- entity_out: float32 [400, 65536], P(None, 'dom')
- relation_out: float32 [400, 256], replicated
Inputs may be any that keep to these rules, and one draw needn't show every extreme that they name: Dom index i is matched with index i XOR plan[0], its partner partition. A device's active edges are its first edge_count slots; in every draw some device uses all 512.
All inputs are finite; a program needn't handle non-finite values.
Results may differ from a plain program's by a relative error of at most 0.0032.
The roundings to bfloat16 on the way count: a program that leaves them out, or rounds other values in their place, can miss the bound.
Values may be sent and summed in bfloat16 or wider, within the bound.
A program may use at most 64 MiB of HBM per device.

v0:
```python
import jax
import jax.numpy as jnp
from jax import lax
from jax.sharding import PartitionSpec as P

entity_rate = 1.0
relation_rate = 0.1


def from_partner(value, axis, stride):
    mask = 2**stride
    pairs = [(source, source ^ mask) for source in range(lax.axis_size(axis))]
    return lax.ppermute(value, axis, pairs)


def complex_parts(values):
    halfway = values.shape[0] // 2
    return (values[:halfway], values[halfway:])


def route_blocks(payload, pattern, bit_order):
    for section_bit in bit_order:
        taken = pattern >> section_bit & 1 == 1
        arrived = from_partner(payload, "dom", section_bit)
        payload = jnp.where(taken, arrived, payload)
    return payload


def return_blocks(payload, pattern, bit_order):
    for section_bit in bit_order:
        taken = pattern >> section_bit & 1 == 1
        arrived = from_partner(payload, "dom", section_bit)
        payload = jnp.where(taken, arrived, payload)
    return payload


def shards(
    entity, relation, head_index, relation_index, tail_index, negative_index, plan, edge_count
):
    highest = lax.Precision.HIGHEST
    features, block_size = entity.shape
    edge_slots = head_index.shape[0]
    negative_slots = negative_index.shape[0]
    sections = lax.axis_size("dom").bit_length() - 1
    bit_order = list(range(sections))
    pattern = plan[0]
    partner = route_blocks(entity.astype(jnp.bfloat16), pattern, bit_order)
    active = (jnp.arange(edge_slots, dtype=jnp.int32) < edge_count[0]).astype(jnp.float32)
    selector = (
        jnp.arange(relation.shape[1], dtype=jnp.int32)[:, None] == relation_index[None, :]
    ).astype(jnp.float32)
    rel_vectors = jnp.dot(relation, selector, precision=highest)
    head_vectors = jnp.take(entity, head_index, axis=1)
    head_real, head_imag = complex_parts(head_vectors)
    rel_real, rel_imag = complex_parts(rel_vectors)
    query = jnp.concatenate(
        [head_real * rel_real - head_imag * rel_imag, head_real * rel_imag + head_imag * rel_real],
        axis=0,
    ).astype(jnp.bfloat16)
    tail_vectors = jnp.take(partner, tail_index, axis=1)
    negative_vectors = jnp.take(partner, negative_index, axis=1)
    positive = jnp.sum(query.astype(jnp.float32) * tail_vectors.astype(jnp.float32), axis=0)
    block_rows = 512

    def score_block(step, carry):
        pull_neg, negative_term = carry
        scores = lax.dot_general(
            query, negative_vectors, (((0,), (0,)), ((), ())), preferred_element_type=jnp.float32
        )
        weights = (jax.nn.sigmoid(scores) * (active / negative_slots)[:, None]).astype(jnp.bfloat16)
        pulled = lax.dot_general(
            negative_vectors, weights, (((1,), (1,)), ((), ())), preferred_element_type=jnp.float32
        )
        pull_neg = pulled
        negative_term = negative_term + lax.dot_general(
            query, weights, (((1,), (0,)), ((), ())), preferred_element_type=jnp.float32
        )
        return (pull_neg, negative_term)

    start_carry = (
        jnp.zeros((features, edge_slots), jnp.float32),
        jnp.zeros((features, negative_slots), jnp.float32),
    )
    pull_neg, negative_term = lax.fori_loop(0, edge_slots // block_rows, score_block, start_carry)
    positive_grad = -jax.nn.sigmoid(-positive) * active
    pull = positive_grad * tail_vectors.astype(jnp.float32) + pull_neg
    pull_real, pull_imag = complex_parts(pull)
    head_term = jnp.concatenate(
        [pull_real * rel_real + pull_imag * rel_imag, pull_imag * rel_real - pull_real * rel_imag],
        axis=0,
    )
    rel_term = jnp.concatenate(
        [
            pull_real * head_real + pull_imag * head_imag,
            pull_imag * head_real - pull_real * head_imag,
        ],
        axis=0,
    )
    tail_term = positive_grad * query.astype(jnp.float32)
    empty = jnp.zeros((features, block_size), jnp.float32)
    head_grad = empty.at[:, head_index].add(head_term)
    partner_grad = empty.at[:, tail_index].add(tail_term).at[:, negative_index].add(negative_term)
    rel_grad = lax.dot_general(
        rel_term,
        selector,
        (((1,), (1,)), ((), ())),
        precision=highest,
        preferred_element_type=jnp.float32,
    )
    rel_total = lax.psum(rel_grad, ("region", "dom"))
    relation_out = relation - relation_rate * rel_total
    returned = return_blocks(partner_grad, pattern, bit_order)
    total_grad = lax.psum(head_grad + returned, "region")
    entity_out = entity - entity_rate * total_grad
    return (entity_out, relation_out)


def solution(mesh):
    in_specs = (
        P(None, "dom"),
        P(),
        P(("region", "dom")),
        P(("region", "dom")),
        P(("region", "dom")),
        P(("region", "dom")),
        P(),
        P(("region", "dom")),
    )
    out_specs = (P(None, "dom"), P())
    return jax.shard_map(shards, mesh=mesh, in_specs=in_specs, out_specs=out_specs, check_vma=False)
```

profile of v0, /device:TPU:1, one launch (start us, length us, event | category | flops | bytes accessed | tf_op | source)
XLA Modules:
  0.0 899.1 jit_solution(6773870561191767479)
XLA Ops:
  8.8 8.7 collective-permute-start
  21.1 13.0 %collective-permute-done.1 = bf16[400,512]{0,1:T(8,128)(2,1)S(1)} collective-permute-done((bf16[400,512]{0,1:T(8,128)(2,1)S(1)}, bf16[400,512]{0,1:T(8,128)(2,1)S(1)}, u32[]{:S(2)}, u32[]{:S(2)}) %collective-permute-start.1) | collective-permute-done | bytes 409632 | tf_op jit(solution)/shard_map/ppermute | solution.py:13
  36.2 25.9 %collective-permute-done.2 = bf16[400,512]{0,1:T(8,128)(2,1)S(1)} collective-permute-done((bf16[400,512]{0,1:T(8,128)(2,1)S(1)}, bf16[400,512]{0,1:T(8,128)(2,1)S(1)}, u32[]{:S(2)}, u32[]{:S(2)}) %collective-permute-start.2) | collective-permute-done | bytes 409632 | tf_op jit(solution)/shard_map/ppermute | solution.py:13
  64.2 12.9 %collective-permute-done.3 = bf16[400,512]{0,1:T(8,128)(2,1)S(1)} collective-permute-done((bf16[400,512]{0,1:T(8,128)(2,1)S(1)}, bf16[400,512]{0,1:T(8,128)(2,1)S(1)}, u32[]{:S(2)}, u32[]{:S(2)}) %collective-permute-start.3) | collective-permute-done | bytes 409632 | tf_op jit(solution)/shard_map/ppermute | solution.py:13
  79.8 13.0 %collective-permute-done.4 = bf16[400,512]{0,1:T(8,128)(2,1)S(1)} collective-permute-done((bf16[400,512]{0,1:T(8,128)(2,1)S(1)}, bf16[400,512]{0,1:T(8,128)(2,1)S(1)}, u32[]{:S(2)}, u32[]{:S(2)}) %collective-permute-start.4) | collective-permute-done | bytes 409632 | tf_op jit(solution)/shard_map/ppermute | solution.py:13
  99.5 6.6 collective-permute-done.5
  108.3 11.6 %collective-permute-done.6 = bf16[400,512]{0,1:T(8,128)(2,1)S(1)} collective-permute-done((bf16[400,512]{0,1:T(8,128)(2,1)S(1)}, bf16[400,512]{0,1:T(8,128)(2,1)S(1)}, u32[]{:S(2)}, u32[]{:S(2)}) %collective-permute-start.6) | collective-permute-done | bytes 409632 | tf_op jit(solution)/shard_map/ppermute | solution.py:13
  120.0 4.7 gather_fusion.2
  126.8 2.7 fusion.4
  132.5 3.8 scatter_custom_fusion
  136.3 10.8 %scatter_fusion = f32[400,512]{0,1:T(8,128)S(1)} fusion(f32[400,512]{0,1:T(8,128)S(1)} %scatter_custom_fusion, s32[1152]{0:T(1024)S(1)} %compare_select_fusion, f32[1152,400]{1,0:T(8,128)} %fusion.19), kind=kCustom, calls=%fused_computation.4 | custom fusion | flops 460800 | bytes 5534208 | tf_op jit(solution)/shard_map/scatter-add | solution.py:102
  148.4 5.8 collective-permute-start.7
  162.2 19.6 %collective-permute-done.8 = f32[400,512]{1,0:T(8,128)S(1)} collective-permute-done((f32[400,512]{1,0:T(8,128)}, f32[400,512]{1,0:T(8,128)S(1)}, u32[]{:S(2)}, u32[]{:S(2)}) %collective-permute-start.8) | collective-permute-done | bytes 819232 | tf_op jit(solution)/shard_map/ppermute | solution.py:13
  186.5 38.8 %collective-permute-done.9 = f32[400,512]{1,0:T(8,128)S(1)} collective-permute-done((f32[400,512]{1,0:T(8,128)}, f32[400,512]{1,0:T(8,128)S(1)}, u32[]{:S(2)}, u32[]{:S(2)}) %collective-permute-start.9) | collective-permute-done | bytes 819232 | tf_op jit(solution)/shard_map/ppermute | solution.py:13
  229.2 2.7 collective-permute-start.10
  231.9 18.6 %collective-permute-done.10 = f32[400,512]{1,0:T(8,128)S(1)} collective-permute-done((f32[400,512]{1,0:T(8,128)}, f32[400,512]{1,0:T(8,128)S(1)}, u32[]{:S(2)}, u32[]{:S(2)}) %collective-permute-start.10) | collective-permute-done | bytes 819232 | tf_op jit(solution)/shard_map/ppermute | solution.py:13
  253.3 2.5 collective-permute-start.11
  255.8 19.6 %collective-permute-done.11 = f32[400,512]{1,0:T(8,128)S(1)} collective-permute-done((f32[400,512]{1,0:T(8,128)}, f32[400,512]{1,0:T(8,128)S(1)}, u32[]{:S(2)}, u32[]{:S(2)}) %collective-permute-start.11) | collective-permute-done | bytes 819232 | tf_op jit(solution)/shard_map/ppermute | solution.py:13
  280.2 17.5 %collective-permute-done.12 = f32[400,512]{1,0:T(8,128)S(1)} collective-permute-done((f32[400,512]{1,0:T(8,128)}, f32[400,512]{1,0:T(8,128)S(1)}, u32[]{:S(2)}, u32[]{:S(2)}) %collective-permute-start.12) | collective-permute-done | bytes 819232 | tf_op jit(solution)/shard_map/ppermute | solution.py:13
  309.8 11.2 %collective-permute-done.13 = f32[400,512]{1,0:T(8,128)} collective-permute-done((f32[400,512]{1,0:T(8,128)}, f32[400,512]{1,0:T(8,128)}, u32[]{:S(2)}, u32[]{:S(2)}) %collective-permute-start.13) | collective-permute-done | bytes 819232 | tf_op jit(solution)/shard_map/ppermute | solution.py:13
  321.0 2.5 copy.38
  323.7 4.9 scatter_fusion.1
  329.6 442.7 %all-reduce.5.cloned.1.call-done = f32[400,256]{1,0:T(8,128)} async-done(((f32[400,256]{1,0:T(8,128)}), f32[400,256]{1,0:T(8,128)}) %all-reduce.5.cloned.1.call-update) | async-done | bytes 409616 | tf_op jit(solution)/shard_map/psum | solution.py:110
  774.2 115.4 %all-reduce.3.cloned.1.call-done = f32[400,512]{0,1:T(8,128)} async-done(((f32[400,512]{0,1:T(8,128)}), f32[400,512]{0,1:T(8,128)}) %all-reduce.3.cloned.1.call-update) | async-done | bytes 819216 | tf_op jit(solution)/shard_map/psum | solution.py:113
  (103 shorter events, 67.4 us)
Async XLA Ops:
  7.2 765.2 %all-reduce.5.cloned.1.call-start = ((), (), s32[]{:S(2)}) async-start(), calls=%async_computation.1 | async-start | bytes 819200 | tf_op jit(solution)/shard_map/psum | solution.py:110
  8.8 12.3 %copy-start.12 = (s32[512]{0:T(512)S(1)}, s32[512]{0:T(512)}, u32[]{:S(2)}) copy-start(s32[512]{0:T(512)} %param.10) | copy-start | bytes 6148
  8.8 10.3 %collective-permute-start = (bf16[400,512]{0,1:T(8,128)(2,1)S(1)}, bf16[400,512]{0,1:T(8,128)(2,1)S(1)}, u32[]{:S(2)}, u32[]{:S(2)}) collective-permute-start(bf16[400,512]{0,1:T(8,128)(2,1)S(1)} %convert_element_type.20), channel_id=1, source_target_pairs={{0,1},{1,0},{2,3},{3,2},{4,5},{5,4},{6,7},{7,6},{8,9},{9,8},{10,11... | collective-permute-start | bytes 1228808 | tf_op jit(solution)/shard_map/ppermute | solution.py:13
  19.1 17.0 %copy-start.13 = (s32[512]{0:T(512)S(1)}, s32[512]{0:T(512)}, u32[]{:S(2)}) copy-start(s32[512]{0:T(512)} %param.12) | copy-start | bytes 6148
  19.1 17.0 %copy-start.10 = (s32[1152]{0:T(1024)S(1)}, s32[1152]{0:T(1024)}, u32[]{:S(2)}) copy-start(s32[1152]{0:T(1024)} %param.13) | copy-start | bytes 13828
  19.1 15.0 %collective-permute-start.1 = (bf16[400,512]{0,1:T(8,128)(2,1)S(1)}, bf16[400,512]{0,1:T(8,128)(2,1)S(1)}, u32[]{:S(2)}, u32[]{:S(2)}) collective-permute-start(bf16[400,512]{0,1:T(8,128)(2,1)S(1)} %broadcast_select_fusion.2), channel_id=1, source_target_pairs={{0,2},{1,3},{2,0},{3,1},{4,6},{5,7},{6,4},{7,5},{8,10},{9,11},{10,... | collective-permute-start | bytes 1228808 | tf_op jit(solution)/shard_map/ppermute | solution.py:13
  34.2 27.9 %collective-permute-start.2 = (bf16[400,512]{0,1:T(8,128)(2,1)S(1)}, bf16[400,512]{0,1:T(8,128)(2,1)S(1)}, u32[]{:S(2)}, u32[]{:S(2)}) collective-permute-start(bf16[400,512]{0,1:T(8,128)(2,1)S(1)} %broadcast_select_fusion.4), channel_id=1, source_target_pairs={{0,4},{1,5},{2,6},{3,7},{4,0},{5,1},{6,2},{7,3},{8,12},{9,13},{10,... | collective-permute-start | bytes 1228808 | tf_op jit(solution)/shard_map/ppermute | solution.py:13
  62.1 17.0 %copy-start.7 = (f32[400,256]{1,0:T(8,128)S(1)}, f32[400,256]{1,0:T(8,128)}, u32[]{:S(2)}) copy-start(f32[400,256]{1,0:T(8,128)} %param.9) | copy-start | bytes 1228804
  62.1 17.0 %copy-start.11 = (s32[512]{0:T(512)S(1)}, s32[512]{0:T(512)}, u32[]{:S(2)}) copy-start(s32[512]{0:T(512)} %param.11) | copy-start | bytes 6148
  62.2 15.0 %collective-permute-start.3 = (bf16[400,512]{0,1:T(8,128)(2,1)S(1)}, bf16[400,512]{0,1:T(8,128)(2,1)S(1)}, u32[]{:S(2)}, u32[]{:S(2)}) collective-permute-start(bf16[400,512]{0,1:T(8,128)(2,1)S(1)} %broadcast_select_fusion.6), channel_id=1, source_target_pairs={{0,8},{1,9},{2,10},{3,11},{4,12},{5,13},{6,14},{7,15},{8,0},{9,1},... | collective-permute-start | bytes 1228808 | tf_op jit(solution)/shard_map/ppermute | solution.py:13
  77.2 15.5 %collective-permute-start.4 = (bf16[400,512]{0,1:T(8,128)(2,1)S(1)}, bf16[400,512]{0,1:T(8,128)(2,1)S(1)}, u32[]{:S(2)}, u32[]{:S(2)}) collective-permute-start(bf16[400,512]{0,1:T(8,128)(2,1)S(1)} %broadcast_select_fusion.8), channel_id=1, source_target_pairs={{0,16},{1,17},{2,18},{3,19},{4,20},{5,21},{6,22},{7,23},{8,24},{9,... | collective-permute-start | bytes 1228808 | tf_op jit(solution)/shard_map/ppermute | solution.py:13
  79.7 28.4 %copy-start.1 = (f32[400,512]{1,0:T(8,128)}, f32[400,512]{1,0:T(8,128)S(1)}, u32[]{:S(2)}) copy-start(f32[400,512]{1,0:T(8,128)S(1)} %convolution_bitcast_fusion) | copy-start | bytes 2457604
  92.8 13.3 %collective-permute-start.5 = (bf16[400,512]{0,1:T(8,128)(2,1)S(1)}, bf16[400,512]{0,1:T(8,128)(2,1)}, u32[]{:S(2)}, u32[]{:S(2)}) collective-permute-start(bf16[400,512]{0,1:T(8,128)(2,1)S(1)} %broadcast_select_fusion.10), channel_id=1, source_target_pairs={{0,32},{1,33},{2,34},{3,35},{4,36},{5,37},{6,38},{7,39},{8,40},{9,... | collective-permute-start | bytes 1228808 | tf_op jit(solution)/shard_map/ppermute | solution.py:13
  99.5 8.9 copy-start.3
  106.1 13.8 %collective-permute-start.6 = (bf16[400,512]{0,1:T(8,128)(2,1)S(1)}, bf16[400,512]{0,1:T(8,128)(2,1)S(1)}, u32[]{:S(2)}, u32[]{:S(2)}) collective-permute-start(bf16[400,512]{0,1:T(8,128)(2,1)S(1)} %broadcast_select_fusion.12), channel_id=1, source_target_pairs={{0,64},{1,65},{2,66},{3,67},{4,68},{5,69},{6,70},{7,71},{8,72},{9,... | collective-permute-start | bytes 1228808 | tf_op jit(solution)/shard_map/ppermute | solution.py:13
  148.4 8.0 collective-permute-start.7
  160.3 21.5 %collective-permute-start.8 = (f32[400,512]{1,0:T(8,128)}, f32[400,512]{1,0:T(8,128)S(1)}, u32[]{:S(2)}, u32[]{:S(2)}) collective-permute-start(f32[400,512]{1,0:T(8,128)} %copy.27), channel_id=1, source_target_pairs={{0,2},{1,3},{2,0},{3,1},{4,6},{5,7},{6,4},{7,5},{8,10},{9,11},{10,... | collective-permute-start | bytes 2457608 | tf_op jit(solution)/shard_map/ppermute | solution.py:13
  184.6 40.7 %collective-permute-start.9 = (f32[400,512]{1,0:T(8,128)}, f32[400,512]{1,0:T(8,128)S(1)}, u32[]{:S(2)}, u32[]{:S(2)}) collective-permute-start(f32[400,512]{1,0:T(8,128)} %copy.29), channel_id=1, source_target_pairs={{0,4},{1,5},{2,6},{3,7},{4,0},{5,1},{6,2},{7,3},{8,12},{9,13},{10,... | collective-permute-start | bytes 2457608 | tf_op jit(solution)/shard_map/ppermute | solution.py:13
  229.2 21.4 %collective-permute-start.10 = (f32[400,512]{1,0:T(8,128)}, f32[400,512]{1,0:T(8,128)S(1)}, u32[]{:S(2)}, u32[]{:S(2)}) collective-permute-start(f32[400,512]{1,0:T(8,128)} %copy.31), channel_id=1, source_target_pairs={{0,8},{1,9},{2,10},{3,11},{4,12},{5,13},{6,14},{7,15},{8,0},{9,1},... | collective-permute-start | bytes 2457608 | tf_op jit(solution)/shard_map/ppermute | solution.py:13
  253.3 22.0 %collective-permute-start.11 = (f32[400,512]{1,0:T(8,128)}, f32[400,512]{1,0:T(8,128)S(1)}, u32[]{:S(2)}, u32[]{:S(2)}) collective-permute-start(f32[400,512]{1,0:T(8,128)} %copy.33), channel_id=1, source_target_pairs={{0,16},{1,17},{2,18},{3,19},{4,20},{5,21},{6,22},{7,23},{8,24},{9,... | collective-permute-start | bytes 2457608 | tf_op jit(solution)/shard_map/ppermute | solution.py:13
  278.0 19.7 %collective-permute-start.12 = (f32[400,512]{1,0:T(8,128)}, f32[400,512]{1,0:T(8,128)S(1)}, u32[]{:S(2)}, u32[]{:S(2)}) collective-permute-start(f32[400,512]{1,0:T(8,128)} %copy.35), channel_id=1, source_target_pairs={{0,32},{1,33},{2,34},{3,35},{4,36},{5,37},{6,38},{7,39},{8,40},{9,... | collective-permute-start | bytes 2457608 | tf_op jit(solution)/shard_map/ppermute | solution.py:13
  300.4 20.6 %collective-permute-start.13 = (f32[400,512]{1,0:T(8,128)}, f32[400,512]{1,0:T(8,128)}, u32[]{:S(2)}, u32[]{:S(2)}) collective-permute-start(f32[400,512]{1,0:T(8,128)} %copy.37), channel_id=1, source_target_pairs={{0,64},{1,65},{2,66},{3,67},{4,68},{5,69},{6,70},{7,71},{8,72},{9,... | collective-permute-start | bytes 2457608 | tf_op jit(solution)/shard_map/ppermute | solution.py:13
  307.4 582.2 %all-reduce.3.cloned.1.call-start = ((), (), s32[]{:S(2)}) async-start(), calls=%async_computation | async-start | bytes 2097152 | tf_op jit(solution)/shard_map/psum | solution.py:113
  328.6 443.8 %copy-start.8 = (f32[400,256]{1,0:T(8,128)S(1)}, f32[400,256]{1,0:T(8,128)}, u32[]{:S(2)}) copy-start(f32[400,256]{1,0:T(8,128)} %param.9) | copy-start | bytes 1228804
  (6 other events, 20.6 us)
Sparse Core Ops, SparseCore 0:
  307.5 464.8 all-reduce.4
  775.3 114.2 all-reduce.2
where the time goes:
time: 900 us; the launch traced here: 899 us
  waiting for transfers between devices  770 us (86%)
  starting transfers between devices  39.6 us (4%)
  local copies, waits for them, and re-layouts  33.7 us (4%)
  other arithmetic  31.1 us (3%)
  between operations  15.9 us (2%)
  matrix products  9.3 us (1%)
    psum x1, waiting for transfers between devices, shards(): rel_total = lax.psum(rel_grad, ('region', 'dom'))  443 us
    ppermute x14, waiting for transfers between devices, from_partner(): return lax.ppermute(value, axis, pairs)  211 us
    psum x1, waiting for transfers between devices, shards(): total_grad = lax.psum(head_grad + returned, 'region')  115 us
    ppermute x14, starting transfers between devices, from_partner(): return lax.ppermute(value, axis, pairs)  39.5 us
  transfers between devices with their start and end apart: 16, of which 16 were waited for; matrix products, arithmetic and copies ran while one was open for 2% of the time, Pallas kernels for 0%

commit v1 on v0

v1 whole, which is shorter than its diff:
```python
import functools

import jax
import jax.numpy as jnp
from jax import lax
from jax.experimental import pallas as pl
from jax.experimental.pallas import tpu as pltpu
from jax.sharding import PartitionSpec as P

entity_rate = 1.0
relation_rate = 0.1

F32 = jnp.float32
BF16 = jnp.bfloat16
MESH = pl.DeviceIdType.MESH


def move(value, offset):
    if offset == 0:
        return value
    pairs = [(source, source ^ offset) for source in range(lax.axis_size("dom"))]
    return lax.ppermute(value, "dom", pairs)


def route(payload, pattern):
    low = [functools.partial(move, offset=digit) for digit in range(8)]
    high = [functools.partial(move, offset=digit << 3) for digit in range(16)]
    payload = lax.switch(pattern & 7, low, payload)
    return lax.switch(pattern >> 3, high, payload)


def split(value, parts):
    pieces = []
    for _ in range(parts):
        piece = value.astype(BF16)
        pieces.append(piece)
        value = value - piece.astype(F32)
    return pieces


NN = (((1,), (0,)), ((), ()))
NT = (((1,), (1,)), ((), ()))
TN = (((0,), (0,)), ((), ()))


def matmul(pieces, other, dims):
    total = None
    for piece in pieces:
        part = lax.dot_general(piece, other, dims, preferred_element_type=F32)
        total = part if total is None else total + part
    return total


def one_hot(rows, index):
    shape = (rows, index.shape[1])
    return jnp.where(lax.broadcasted_iota(jnp.int32, shape, 0) == index, 1.0, 0.0).astype(BF16)


def terms_kernel(
    count_ref, entity_ref, relation_ref, partner_ref, head_ref, rel_ref, tail_ref, neg_ref,
    head_grad_ref, partner_grad_ref, rel_grad_ref, wide,
):
    features, block = entity_ref.shape
    half = features // 2
    rels = relation_ref.shape[1]
    edges = head_ref.shape[1]
    negatives = neg_ref.shape[1]
    count = count_ref[0]
    head_pick = one_hot(block, head_ref[...])
    rel_pick = one_hot(rels, rel_ref[...])
    tail_pick = one_hot(block, tail_ref[...])
    head = matmul(split(entity_ref[...], 3), head_pick, NN)
    rel = matmul(split(relation_ref[...], 3), rel_pick, NN)
    head_real, head_imag = head[:half], head[half:]
    rel_real, rel_imag = rel[:half], rel[half:]
    wide[:half, :] = head_real * rel_real - head_imag * rel_imag
    wide[half:, :] = head_real * rel_imag + head_imag * rel_real
    query = wide[...].astype(BF16)
    query_wide = query.astype(F32)
    neg_pick = one_hot(block, neg_ref[...])
    times = lax.dot_general(
        jnp.ones((8, negatives), BF16), neg_pick, NT, preferred_element_type=F32
    )[:1]

    partner = partner_ref[...]
    tail = lax.dot_general(partner, tail_pick, NN, preferred_element_type=F32)
    active = jnp.where(lax.broadcasted_iota(jnp.int32, (1, edges), 1) < count, 1.0, 0.0)
    positive = jnp.sum(query_wide * tail, axis=0, keepdims=True)
    positive_grad = -jax.nn.sigmoid(-positive) * active
    scores = lax.dot_general(query, partner, TN, preferred_element_type=F32)
    share = jnp.where(
        lax.broadcasted_iota(jnp.int32, (edges, 1), 0) < count, 1.0 / negatives, 0.0
    )
    weights = (jax.nn.sigmoid(scores) * share).astype(BF16).astype(F32) * times
    weight_hi, weight_lo = split(weights, 2)
    pull = (
        positive_grad * tail
        + lax.dot_general(partner, weight_hi, NT, preferred_element_type=F32)
        + lax.dot_general(partner, weight_lo, NT, preferred_element_type=F32)
    )
    partner_grad = (
        lax.dot_general(query, weight_hi, NN, preferred_element_type=F32)
        + lax.dot_general(query, weight_lo, NN, preferred_element_type=F32)
        + matmul(split(positive_grad * query_wide, 2), tail_pick, NT)
    )
    partner_grad_ref[...] = partner_grad.astype(BF16)
    pull_real, pull_imag = pull[:half], pull[half:]
    wide[:half, :] = pull_real * head_real + pull_imag * head_imag
    wide[half:, :] = pull_imag * head_real - pull_real * head_imag
    rel_grad_ref[:features, :] = matmul(split(wide[...], 2), rel_pick, NT)
    rel_grad_ref[features:, :] = jnp.zeros((rel_grad_ref.shape[0] - features, rels), F32)
    wide[:half, :] = pull_real * rel_real + pull_imag * rel_imag
    wide[half:, :] = pull_imag * rel_real - pull_real * rel_imag
    head_grad_ref[...] = matmul(split(wide[...], 2), head_pick, NT)


def edge_terms(edge_count, entity, relation, partner, head, rel, tail, neg):
    features, block = entity.shape
    vmem = pl.BlockSpec(memory_space=pltpu.VMEM)
    return pl.pallas_call(
        terms_kernel,
        out_shape=(
            jax.ShapeDtypeStruct((features, block), F32),
            jax.ShapeDtypeStruct((features, block), BF16),
            jax.ShapeDtypeStruct((512, relation.shape[1]), F32),
        ),
        in_specs=[pl.BlockSpec(memory_space=pltpu.SMEM)] + [vmem] * 7,
        out_specs=(vmem, vmem, vmem),
        scratch_shapes=[pltpu.VMEM((features, head.shape[1]), F32)],
        name="edge_terms",
    )(edge_count, entity, relation, partner, head, rel, tail, neg)


def sums_kernel(
    entity_ref, relation_ref, head_ref, returned_ref, rel_ref,
    entity_out, relation_out,
    mine, sent, got, shared,
    core_got, core_sum, x_got, x_sum, y_got, lo_all, hi_all, whole,
    send_sem, recv_sem,
):
    features = relation_ref.shape[0]
    quarter = entity_ref.shape[1] // 4
    region = lax.axis_index("region")
    dom = lax.axis_index("dom")
    x = dom // 32
    y = lax.rem(dom // 8, 4)
    z = lax.rem(dom // 2, 4)
    core = lax.rem(dom, 2)

    def at(region=region, x=x, y=y, z=z, core=core):
        return (region, ((x * 4 + y) * 4 + z) * 2 + core)

    def turn(value, step):
        return lax.rem(value + step, 4)

    def peer(axis, step):
        if axis == "core":
            return at(core=1 - core)
        if axis == "x":
            return at(x=turn(x, step))
        if axis == "y":
            return at(y=turn(y, step))
        if axis == "z":
            return at(z=turn(z, step))
        return at(region=turn(region, step))

    barrier = pltpu.get_barrier_semaphore()
    peers = [peer("core", 1)] + [peer(a, s) for a in ("x", "y", "z", "r") for s in (1, 2, 3)]
    for other in peers:
        pl.semaphore_signal(barrier, inc=1, device_id=other, device_id_type=MESH)

    for q in range(4):
        columns = slice(q * quarter, (q + 1) * quarter)
        value = head_ref[:, columns] + returned_ref[:, columns].astype(F32)
        mine[q] = value
        sent[q] = value.astype(BF16)

    pl.semaphore_wait(barrier, len(peers))
    used = [0]

    def send(src, dst, device):
        slot = used[0]
        used[0] += 1
        copy = pltpu.make_async_remote_copy(
            src_ref=src,
            dst_ref=dst,
            send_sem=send_sem.at[slot],
            recv_sem=recv_sem.at[slot],
            device_id=device,
            device_id_type=MESH,
        )
        copy.start()
        return copy

    def wait(copies):
        for copy in copies:
            copy.wait()

    steps = (2, 1, 3)
    entity_copies = [
        send(sent.at[turn(region, s)], got.at[s - 1], peer("r", s)) for s in steps
    ]

    wait([send(rel_ref.at[1 - core], core_got, peer("core", 1))])
    core_sum[...] = rel_ref[core] + core_got[...]
    wait([send(core_sum.at[turn(x, s)], x_got.at[s - 1], peer("x", s)) for s in steps])
    x_sum[...] = core_sum[x] + x_got[0] + x_got[1] + x_got[2]
    wait([send(x_sum.at[turn(y, s)], y_got.at[s - 1], peer("y", s)) for s in steps])
    lo_all[z] = x_sum[y] + y_got[0] + y_got[1] + y_got[2]
    wait([send(lo_all.at[z], lo_all.at[z], peer("z", s)) for s in steps])
    hi_all[region] = lo_all[0] + lo_all[1] + lo_all[2] + lo_all[3]
    wait([send(hi_all.at[region], hi_all.at[region], peer("r", s)) for s in steps])
    whole[core, x, y] = hi_all[0] + hi_all[1] + hi_all[2] + hi_all[3]

    wait(entity_copies)
    total = mine[region] + got[0].astype(F32) + got[1].astype(F32) + got[2].astype(F32)
    shared[region] = total.astype(BF16)
    entity_copies = [send(shared.at[region], shared.at[region], peer("r", s)) for s in steps]

    wait([send(whole.at[core, x, y], whole.at[core, x, y], peer("y", s)) for s in steps])
    wait([send(whole.at[core, x], whole.at[core, x], peer("x", s)) for s in steps])
    wait([send(whole.at[core], whole.at[core], peer("core", 1))])
    for piece in range(features // 16):
        rows = slice(piece * 16, piece * 16 + 16)
        part = whole[piece // 16, piece // 4 % 4, piece % 4]
        relation_out[rows, :] = relation_ref[rows, :] - relation_rate * part

    wait(entity_copies)
    for q in range(4):
        columns = slice(q * quarter, (q + 1) * quarter)
        entity_out[:, columns] = entity_ref[:, columns] - entity_rate * shared[q].astype(F32)


def sum_all(entity, relation, head_grad, returned, rel_grad):
    features, block = entity.shape
    rels = relation.shape[1]
    quarter = block // 4
    vmem = pl.BlockSpec(memory_space=pltpu.VMEM)
    piece = (16, rels)
    copies = 26
    return pl.pallas_call(
        sums_kernel,
        out_shape=(
            jax.ShapeDtypeStruct(entity.shape, F32),
            jax.ShapeDtypeStruct(relation.shape, F32),
        ),
        in_specs=[vmem] * 5,
        out_specs=(vmem, vmem),
        scratch_shapes=[
            pltpu.VMEM((4, features, quarter), F32),
            pltpu.VMEM((4, features, quarter), BF16),
            pltpu.VMEM((3, features, quarter), BF16),
            pltpu.VMEM((4, features, quarter), BF16),
            pltpu.VMEM((4, 4) + piece, F32),
            pltpu.VMEM((4, 4) + piece, F32),
            pltpu.VMEM((3, 4) + piece, F32),
            pltpu.VMEM((4,) + piece, F32),
            pltpu.VMEM((3,) + piece, F32),
            pltpu.VMEM((4,) + piece, F32),
            pltpu.VMEM((4,) + piece, F32),
            pltpu.VMEM((2, 4, 4) + piece, F32),
            pltpu.SemaphoreType.DMA((copies,)),
            pltpu.SemaphoreType.DMA((copies,)),
        ],
        compiler_params=pltpu.CompilerParams(collective_id=0, has_side_effects=True),
        name="sum_all",
    )(entity, relation, head_grad, returned, rel_grad.reshape((2, 4, 4) + piece))


def shards(
    entity, relation, head_index, relation_index, tail_index, negative_index, plan, edge_count
):
    pattern = plan[0]
    partner = route(entity.astype(BF16), pattern)
    head_grad, partner_grad, rel_grad = edge_terms(
        edge_count,
        entity,
        relation,
        partner,
        head_index[None, :],
        relation_index[None, :],
        tail_index[None, :],
        negative_index[None, :],
    )
    returned = route(partner_grad, pattern)
    return sum_all(entity, relation, head_grad, returned, rel_grad)


def solution(mesh):
    in_specs = (
        P(None, "dom"),
        P(),
        P(("region", "dom")),
        P(("region", "dom")),
        P(("region", "dom")),
        P(("region", "dom")),
        P(),
        P(("region", "dom")),
    )
    out_specs = (P(None, "dom"), P())
    return jax.shard_map(shards, mesh=mesh, in_specs=in_specs, out_specs=out_specs, check_vma=False)
```

time: 900 us -> 107 us (0.12)
  waiting for transfers between devices: 770 us -> 11.2 us
  Pallas kernels: 0 us -> 79 us
  starting transfers between devices: 39.6 us -> 8.93 us
  other arithmetic: 31.1 us -> 1.2 us
  local copies, waits for them, and re-layouts: 33.7 us -> 4.23 us
  between operations: 15.9 us -> 1.99 us
  matrix products: 9.3 us -> 0 us
    psum x2 -> x0, waiting for transfers between devices: 558 us -> none  [the longest x1 443 us: shards(): rel_total = lax.psum(rel_grad, ('region', 'dom'))]
    ppermute x14 -> x2, waiting for transfers between devices: 211 us -> 11.2 us  [move(): return lax.ppermute(value, 'dom', pairs)]
    pallas_call x0 -> x2, Pallas kernels: none -> 79 us  [the longest x1 72.3 us: sum_all(): pl.pallas_call(sums_kernel, out_shape=(jax.ShapeDtypeStruct(entity.shape,...]
    ppermute x14 -> x2, starting transfers between devices: 39.5 us -> 8.93 us  [move(): return lax.ppermute(value, 'dom', pairs)]
    scatter-add x3 -> x0, other arithmetic: 19.6 us -> none  [the longest x2 14.7 us: shards(): empty.at[:, tail_index].add(tail_term).at[:, negative_index]]
    ppermute x7 -> x0, local copies, waits for them, and re-layouts: 10.3 us -> none  [from_partner(): return lax.ppermute(value, axis, pairs)]
    gather x5 -> x0, local copies, waits for them, and re-layouts: 9.64 us -> none  [the longest x1 4.67 us: shards(): negative_vectors = jnp.take(partner, negative_index, axis=1)]
    dot_general x5 -> x0, matrix products: 9.3 us -> none  [the longest x1 2.72 us: score_block(): lax.dot_general(query, negative_vectors, (((0,), (0,)), ((), ())), prefer...]
  transfers between devices with their start and end apart: 16 -> 2, of which waited for: 16 -> 2; matrix products, arithmetic and copies ran while one was open for 2% -> 0% of each run, Pallas kernels for 0% -> 0%
where the time goes in v1:
time: 107 us
  Pallas kernels  79 us (74%)
  waiting for transfers between devices  11.2 us (10%)
  starting transfers between devices  8.93 us (8%)
  local copies, waits for them, and re-layouts  4.23 us (4%)
  between operations  1.99 us (2%)
  other arithmetic  1.2 us (1%)
    pallas_call x1, Pallas kernels, sum_all(): pl.pallas_call(sums_kernel, out_shape=(jax.ShapeDtypeStruct(entity.shape,...  72.3 us
    ppermute x2, waiting for transfers between devices, move(): return lax.ppermute(value, 'dom', pairs)  11.2 us
    ppermute x2, starting transfers between devices, move(): return lax.ppermute(value, 'dom', pairs)  8.93 us
    pallas_call x1, Pallas kernels, edge_terms(): pl.pallas_call(terms_kernel, out_shape=(jax.ShapeDtypeStruct((features, b...  6.74 us
    unnamed x6, local copies, waits for them, and re-layouts  3.58 us
  transfers between devices with their start and end apart: 2, of which 2 were waited for; matrix products, arithmetic and copies ran while one was open for 0% of the time, Pallas kernels for 0%

profile of v1, /device:TPU:1, one launch (start us, length us, event | category | flops | bytes accessed | tf_op | source)
XLA Modules:
  0.0 106.8 jit_solution(1354122775556448916)
XLA Ops:
  1.9 0.0 copy-start.1
  1.9 0.7 copy-done.1
  2.6 0.6 broadcast_in_dim.15.neg_ref
  3.2 1.2 %convert_element_type.27 = bf16[400,512]{1,0:T(8,128)(2,1)S(1)} convert(f32[400,512]{1,0:T(8,128)} %entity_ref.3) | non-fusion elementwise | flops 204800 | bytes 1228800 | tf_op jit(solution)/shard_map/convert_element_type | solution.py:274
  4.4 10.6 %conditional.4 = (bf16[400,512]{1,0:T(8,128)(2,1)S(1)}) conditional(s32[]{:T(128)} %bitcast.1, bf16[400,512]{1,0:T(8,128)(2,1)S(1)} %convert_element_type.27, bf16[400,512]{1,0:T(8,128)(2,1)S(1)} %convert_element_type.27, bf16[400,512]{1,0:T(8,128)(2,1)S(1)} %convert_element_type.27, ...), branch_computations={%region_0.0_spmd, %region_1.0_spmd, %region_2.0_spmd, %region_3.0_... | conditional | bytes 2457648 | solution.py:28
  4.5 4.9 %collective-permute-start.2 = (bf16[400,512]{1,0:T(8,128)(2,1)S(1)}, bf16[400,512]{1,0:T(8,128)(2,1)S(1)}, u32[]{:S(2)}, u32[]{:S(2)}) collective-permute-start(bf16[400,512]{1,0:T(8,128)(2,1)S(1)} %param.3), channel_id=1, source_target_pairs={{0,3},{1,2},{2,1},{3,0},{4,7},{5,6},{6,5},{7,4},{8,11},{9,10},{10,... | collective-permute-start | bytes 1228808 | tf_op jit(solution)/shard_map/cond/branch_3_fun/ppermute | solution.py:22
  9.4 5.6 %collective-permute-done.2 = bf16[400,512]{1,0:T(8,128)(2,1)S(1)} collective-permute-done((bf16[400,512]{1,0:T(8,128)(2,1)S(1)}, bf16[400,512]{1,0:T(8,128)(2,1)S(1)}, u32[]{:S(2)}, u32[]{:S(2)}) %collective-permute-start.2) | collective-permute-done | bytes 409632 | tf_op jit(solution)/shard_map/cond/branch_3_fun/ppermute | solution.py:22
  15.1 6.7 %edge_terms.1 = (f32[400,512]{1,0:T(8,128)}, bf16[400,512]{1,0:T(8,128)(2,1)S(1)}, f32[512,256]{1,0:T(8,128)}) custom-call(s32[1]{0:T(128)S(6)} %copy.61.count_ref, f32[400,512]{1,0:T(8,128)} %entity_ref.3, f32[400,256]{1,0:T(8,128)} %relation_ref.3, bf16[400,512]{1,0:T(8,128)(2,1)S(1)} %get-tuple-element.113.partner_ref, s32[1,512]{1,0:T(1,128)} %bitcast.7, ...), custom_call_target="tpu_custom_call" | custom-call | tf_op jit(solution)/shard_map/edge_terms/pallas_call | solution.py:120
  21.8 9.7 %conditional.6 = (bf16[400,512]{1,0:T(8,128)(2,1)S(1)}) conditional(s32[]{:T(128)} %bitcast.1, bf16[400,512]{1,0:T(8,128)(2,1)S(1)} %get-tuple-element.106, bf16[400,512]{1,0:T(8,128)(2,1)S(1)} %get-tuple-element.106, bf16[400,512]{1,0:T(8,128)(2,1)S(1)} %get-tuple-element.106, ...), branch_computations={%region_24.0_spmd, %region_25.0_spmd, %region_26.0_spmd, %region_2... | conditional | bytes 2457648 | solution.py:28
  21.8 4.0 %collective-permute-start.24 = (bf16[400,512]{1,0:T(8,128)(2,1)S(1)}, bf16[400,512]{1,0:T(8,128)(2,1)S(1)}, u32[]{:S(2)}, u32[]{:S(2)}) collective-permute-start(bf16[400,512]{1,0:T(8,128)(2,1)S(1)} %param.27), channel_id=1, source_target_pairs={{0,3},{1,2},{2,1},{3,0},{4,7},{5,6},{6,5},{7,4},{8,11},{9,10},{10,... | collective-permute-start | bytes 1228808 | tf_op jit(solution)/shard_map/cond/branch_3_fun/ppermute | solution.py:22
  25.9 5.6 %collective-permute-done.24 = bf16[400,512]{1,0:T(8,128)(2,1)S(1)} collective-permute-done((bf16[400,512]{1,0:T(8,128)(2,1)S(1)}, bf16[400,512]{1,0:T(8,128)(2,1)S(1)}, u32[]{:S(2)}, u32[]{:S(2)}) %collective-permute-start.24) | collective-permute-done | bytes 409632 | tf_op jit(solution)/shard_map/cond/branch_3_fun/ppermute | solution.py:22
  31.6 72.3 %sum_all.1 = (f32[400,512]{1,0:T(8,128)}, f32[400,256]{1,0:T(8,128)}) custom-call(f32[400,512]{1,0:T(8,128)} %entity_ref.3, f32[400,256]{1,0:T(8,128)} %relation_ref.3, f32[400,512]{1,0:T(8,128)} %get-tuple-element.105.head_ref, bf16[400,512]{1,0:T(8,128)(2,1)S(1)} %get-tuple-element.115.returned_ref, f32[2,4,4,16,256]{4,3,2,1,0:T(8,128)} %bitcast.6), custom_call_target="tpu_custom_call" | custom-call | tf_op jit(solution)/shard_map/sum_all/pallas_call | solution.py:241
  103.9 0.0 copy-start
  103.9 2.1 %copy.62 = f32[400,512]{1,0:T(8,128)} copy(f32[400,512]{1,0:T(8,128)} %get-tuple-element.110) | data formatting | bytes 1638400
  106.0 0.0 copy-done
  106.0 0.8 copy.63
  (4 shorter events, 0.2 us)
Async XLA Ops:
  1.9 0.7 copy-start.1
  4.5 10.6 %collective-permute-start.2 = (bf16[400,512]{1,0:T(8,128)(2,1)S(1)}, bf16[400,512]{1,0:T(8,128)(2,1)S(1)}, u32[]{:S(2)}, u32[]{:S(2)}) collective-permute-start(bf16[400,512]{1,0:T(8,128)(2,1)S(1)} %param.3), channel_id=1, source_target_pairs={{0,3},{1,2},{2,1},{3,0},{4,7},{5,6},{6,5},{7,4},{8,11},{9,10},{10,... | collective-permute-start | bytes 1228808 | tf_op jit(solution)/shard_map/cond/branch_3_fun/ppermute | solution.py:22
  21.8 9.6 %collective-permute-start.24 = (bf16[400,512]{1,0:T(8,128)(2,1)S(1)}, bf16[400,512]{1,0:T(8,128)(2,1)S(1)}, u32[]{:S(2)}, u32[]{:S(2)}) collective-permute-start(bf16[400,512]{1,0:T(8,128)(2,1)S(1)} %param.27), channel_id=1, source_target_pairs={{0,3},{1,2},{2,1},{3,0},{4,7},{5,6},{6,5},{7,4},{8,11},{9,10},{10,... | collective-permute-start | bytes 1228808 | tf_op jit(solution)/shard_map/cond/branch_3_fun/ppermute | solution.py:22
  103.9 2.2 %copy-start = (f32[400,256]{1,0:T(8,128)S(1)}, f32[400,256]{1,0:T(8,128)}, u32[]{:S(2)}) copy-start(f32[400,256]{1,0:T(8,128)} %get-tuple-element.111) | copy-start | bytes 1228804
